TPU v7x, 32 devices: a whole 2x2x4 slice. The times are simulated.
32 devices in a mesh: member: 4 (over y, core), space: 8 (over z, x).
Axes of the slice: x: 2, y: 2, z: 4, core: 2. Of those that a mesh axis runs over, the one named last changes fastest.
Arguments:
- prior_sample: float32 [256, 65536], P('member', 'space'), may hold values from -6 to 6
- measured_point_location: int32 [32, 128], P('space'), may hold values from 0 to 8191
- measured_data: float32 [32, 128], P('space'), may hold values from -12 to 12
- measurement_noise_sigma: float32 [32, 128], P('space'), may hold values from 2 to 64
- measured_slots_used: int32 [8], P('space'), may hold values from 128 to 512, as said below
Outputs:
- analysis: float32 [256, 65536], P('member', 'space')
Inputs may be any that keep to these rules, and one draw needn't show every extreme that they name: measured_slots_used gives for each space block how many of its first slots are in use; some block uses all 512 slots. `measured_point_location`: each index is a state point of the observation's own space block.
All inputs are finite; a program needn't handle non-finite values.
Results may differ from a plain program's by a relative error of at most 0.000088.
Values sent between devices are 32-bit elements; how exact they have to be, the bound alone decides.
A program may use at most 64 MiB of HBM per device.

v0:
```python
import math

import jax
import jax.numpy as jnp
from jax import lax
from jax.sharding import PartitionSpec as P


def solve_lower(lower_factor, target):
    return lax.linalg.triangular_solve(lower_factor, target, left_side=True, lower=True)


def body(
    prior_sample,
    measured_point_location,
    measured_data,
    measurement_noise_sigma,
    measured_slots_used,
):
    exact_arithmetic = lax.Precision.HIGHEST
    anomaly_matrix, points_in_region = prior_sample.shape
    region_batches = lax.axis_size("member")
    sample_total = anomaly_matrix * region_batches
    pointwise_spread = points_in_region // region_batches
    linear_position = measured_point_location.reshape(-1)
    obs_blk = linear_position.shape[0]
    observation_deviation = obs_blk // region_batches
    propagated_grid = jnp.take(prior_sample, linear_position, axis=1).reshape(
        anomaly_matrix, region_batches, observation_deviation
    )
    prior_regions = prior_sample.reshape(anomaly_matrix, region_batches, pointwise_spread)
    prior_sample_full, integrate_dynamics = (
        lax.all_to_all(prior_regions, "member", split_axis=1, concat_axis=0, tiled=True),
        lax.all_to_all(propagated_grid, "member", split_axis=1, concat_axis=0, tiled=True),
    )
    integrate_dynamics = integrate_dynamics.reshape(sample_total, observation_deviation)
    rank = lax.axis_index("member")
    start = rank * observation_deviation
    my_value = lax.dynamic_slice_in_dim(measured_data.reshape(-1), start, observation_deviation)
    my_sigma = lax.dynamic_slice_in_dim(
        measurement_noise_sigma.reshape(-1), start, observation_deviation
    )
    slots = start + jnp.arange(observation_deviation, dtype=jnp.int32)
    valid = slots < measured_slots_used[0]
    weight = jnp.where(valid, 1.0 / my_sigma, jnp.zeros_like(my_sigma))
    sim_mean = jnp.mean(integrate_dynamics, axis=0)
    perturbed = (integrate_dynamics - sim_mean[None, :]) * weight[None, :]
    innovation = (my_value - sim_mean) * weight
    gram_loc = jnp.dot(perturbed, perturbed.T, precision=exact_arithmetic)
    cross_loc = jnp.dot(perturbed, innovation, precision=exact_arithmetic)
    gram_block, cross_block = lax.psum((gram_loc, cross_loc), "member")
    gram_all, cross = lax.psum((gram_block, cross_block), "space")
    cov_matrix = gram_all + (sample_total - 1) * jnp.eye(sample_total, dtype=jnp.float32)
    lower_factor = jnp.linalg.cholesky(cov_matrix)
    inverse = solve_lower(lower_factor, jnp.eye(sample_total, dtype=jnp.float32))
    projected = jnp.dot(inverse, cross, precision=exact_arithmetic)
    mean_weight = jnp.dot(inverse.T, projected, precision=exact_arithmetic)
    weight_matrix_update = math.sqrt(sample_total - 1) * inverse + mean_weight[None, :]
    sample_vectors = prior_sample_full.reshape(sample_total, -1)
    prior_average = jnp.mean(sample_vectors, axis=0)
    updated_sample = prior_average[None, :] + jnp.dot(
        weight_matrix_update, sample_vectors - prior_average[None, :], precision=exact_arithmetic
    )
    returned = lax.all_to_all(
        updated_sample.reshape(prior_sample_full.shape),
        "member",
        split_axis=0,
        concat_axis=1,
        tiled=True,
    )
    return returned.reshape(anomaly_matrix, points_in_region)


def solution(mesh):
    placed = (
        P("member", "space"),
        P("space", None),
        P("space", None),
        P("space", None),
        P("space"),
    )
    return jax.shard_map(
        body, mesh=mesh, in_specs=placed, out_specs=P("member", "space"), check_vma=False
    )
```

profile of v0, /device:TPU:0, one launch (start us, length us, event | category | flops | bytes accessed | tf_op | source)
XLA Modules:
  0.0 247.3 jit_solution(18277730756764225531)
XLA Ops:
  6.5 3.8 %copy.26 = f32[64,8192]{0,1:T(8,128)} copy(f32[64,8192]{1,0:T(8,128)} %param.5) | data formatting | bytes 4194304 | tf_op args[0]
  10.4 3.4 %gather_fusion = f32[512,64]{1,0:T(8,128)S(1)} fusion(f32[64,8192]{0,1:T(8,128)} %copy.26, s32[1024]{0:T(1024)S(1)} %pad_clamp_fusion), kind=kCustom, calls=%fused_computation | custom fusion | bytes 264192 | tf_op jit(solution)/shard_map/jit(_take)/gather | solution.py:28
  14.5 4.3 %all-to-all-start.1 = ((f32[64,4,128]{2,0,1:T(8,128)}), f32[64,4,128]{2,0,1:T(8,128)S(1)}, u32[]{:S(2)}, u32[]{:S(2)}) async-start(f32[64,4,128]{2,0,1:T(8,128)} %broadcast_select_fusion), calls=%async_computation.1 | async-start | bytes 262144 | tf_op jit(solution)/shard_map/all_to_all | solution.py:34
  19.4 1.5 copy.43
  21.7 1.6 all-to-all-done.1
  23.4 3.6 %all-to-all-start = ((f32[64,4,2048]{2,0,1:T(8,128)}), f32[64,4,2048]{2,0,1:T(8,128)S(1)}, u32[]{:S(2)}, u32[]{:S(2)}) async-start(f32[64,4,2048]{2,0,1:T(8,128)} %bitcast.88), calls=%async_computation | async-start | bytes 4194304 | tf_op jit(solution)/shard_map/all_to_all | solution.py:33
  27.1 1.1 fusion.27
  28.3 37.1 %all-reduce.4.cloned.1.call-done = f32[256,256]{0,1:T(8,128)} async-done(((f32[256,256]{0,1:T(8,128)}), f32[256,256]{0,1:T(8,128)}) %all-reduce.4.cloned.1.call-update) | async-done | bytes 262160 | tf_op jit(solution)/shard_map/psum | solution.py:51
  66.3 5.8 %psum.30 = f32[256]{0:T(256)S(1)} all-reduce(f32[256]{0:T(256)S(1)} %bitcast.97), channel_id=1, replica_groups=mesh['member'=4,'space'=8] {'member'}, use_global_device_ids=true, to_apply=%region_8.9 | all-reduce | flops 256 | bytes 2048 | tf_op jit(solution)/shard_map/psum | solution.py:51
  72.1 21.5 %psum.31 = f32[256]{0:T(256)S(1)} all-reduce(f32[256]{0:T(256)S(1)} %psum.30), channel_id=1, replica_groups=mesh['member'=4,'space'=8] {'space'}, use_global_device_ids=true, to_apply=%region_9.10 | all-reduce | flops 256 | bytes 2048 | tf_op jit(solution)/shard_map/psum | solution.py:52
  93.6 46.2 %all-reduce.6.cloned.1.call-done = f32[256,256]{0,1:T(8,128)} async-done(((f32[256,256]{0,1:T(8,128)}), f32[256,256]{0,1:T(8,128)}) %all-reduce.6.cloned.1.call-update) | async-done | bytes 262160 | tf_op jit(solution)/shard_map/psum | solution.py:52
  141.0 1.0 fusion.3
  142.0 11.7 %cholesky.49 = f32[128,128]{1,0:T(8,128)S(1)} custom-call(f32[128,128]{1,0:T(8,128)S(1)} %cholesky.115), custom_call_target="Cholesky" | custom-call | tf_op jit(solution)/shard_map/jit(cholesky)/cholesky | solution.py:54
  153.7 9.8 %custom-call.14 = f32[1,128,128]{1,2,0:T(8,128)S(1)} custom-call(f32[1,128,128]{2,1,0:T(8,128)S(1)} %get-tuple-element.36), custom_call_target="InvertDiagBlocksLowerTriangular" | custom-call | tf_op jit(solution)/shard_map/jit(cholesky)/cholesky | solution.py:54
  164.0 11.7 %cholesky.103 = f32[128,128]{1,0:T(8,128)S(1)} custom-call(f32[128,128]{1,0:T(8,128)S(1)} %convolution_subtract_fusion.1), custom_call_target="Cholesky" | custom-call | tf_op jit(solution)/shard_map/jit(cholesky)/cholesky | solution.py:54
  178.2 4.3 %while.1 = (s32[]{:T(128)}, f32[256,256]{0,1:T(8,128)S(1)}, s32[2,2]{1,0:T(2,128)S(1)}, f32[2,128,128]{2,1,0:T(8,128)S(1)}, s32[]{:T(128)}) while((s32[]{:T(128)}, f32[256,256]{0,1:T(8,128)S(1)}, s32[2,2]{1,0:T(2,128)S(1)}, f32[2,128,128]{2,1,0:T(8,128)S(1)}, s32[]{:T(128)}) %tuple.24), condition=%wide.while_cond, body=%wide.while_body.sunk | while | flops 2 | bytes 393321 | solution.py:10
  178.9 1.3 dynamic-slice.7
  181.0 1.3 dynamic-slice.7
  182.5 19.9 %custom-call.15 = f32[2,128,128]{1,2,0:T(8,128)S(1)} custom-call(f32[2,128,128]{2,1,0:T(8,128)S(1)} %get-tuple-element.12), custom_call_target="InvertDiagBlocksLowerTriangular" | custom-call | tf_op jit(solution)/shard_map/triangular_solve | solution.py:10
  204.3 1.9 fusion
  206.2 2.2 copy.35
  208.4 28.2 %all_to_all.45 = f32[256,1,2048]{2,1,0:T(1,128)S(1)} all-to-all(f32[256,1,2048]{2,1,0:T(1,128)S(1)} %copy.35), channel_id=1, replica_groups=mesh['member'=4,'space'=8] {'member'}, dimensions={0} | all-to-all | bytes 4194304 | tf_op jit(solution)/shard_map/all_to_all | solution.py:64
  236.6 1.4 copy.36
  237.9 2.5 %copy.41 = f32[8,8,4,2048]{3,1,2,0:T(8,128)} copy(f32[8,8,4,2048]{3,2,1,0:T(4,128)S(1)} %bitcast.90) | data formatting | bytes 4194304
  (55 shorter events, 8.9 us)
Async XLA Ops:
  6.5 3.8 %copy-start.1 = (s32[4,128]{1,0:T(4,128)S(1)}, s32[4,128]{1,0:T(4,128)}, u32[]{:S(2)}) copy-start(s32[4,128]{1,0:T(4,128)} %param.6) | copy-start | bytes 6148
  10.3 9.1 %copy-start = (f32[64,8192]{1,0:T(8,128)S(1)}, f32[64,8192]{1,0:T(8,128)}, u32[]{:S(2)}) copy-start(f32[64,8192]{1,0:T(8,128)} %param.5) | copy-start | bytes 6291460
  14.5 8.9 %all-to-all-start.1 = ((f32[64,4,128]{2,0,1:T(8,128)}), f32[64,4,128]{2,0,1:T(8,128)S(1)}, u32[]{:S(2)}, u32[]{:S(2)}) async-start(f32[64,4,128]{2,0,1:T(8,128)} %broadcast_select_fusion), calls=%async_computation.1 | async-start | bytes 262144 | tf_op jit(solution)/shard_map/all_to_all | solution.py:34
  23.4 180.5 %all-to-all-start = ((f32[64,4,2048]{2,0,1:T(8,128)}), f32[64,4,2048]{2,0,1:T(8,128)S(1)}, u32[]{:S(2)}, u32[]{:S(2)}) async-start(f32[64,4,2048]{2,0,1:T(8,128)} %bitcast.88), calls=%async_computation | async-start | bytes 4194304 | tf_op jit(solution)/shard_map/all_to_all | solution.py:33
  27.0 38.4 %all-reduce.4.cloned.1.call-start = ((), (), s32[]{:S(2)}) async-start(), calls=%async_computation.3 | async-start | bytes 524288 | tf_op jit(solution)/shard_map/psum | solution.py:51
  28.2 111.6 %all-reduce.6.cloned.1.call-start = ((), (), s32[]{:S(2)}) async-start(), calls=%async_computation.4 | async-start | bytes 524288 | tf_op jit(solution)/shard_map/psum | solution.py:52
Sparse Core Ops, SparseCore 0:
  30.1 35.2 all-reduce.3
  68.7 71.0 all-reduce.5
where the time goes:
time: 248 us; the launch traced here: 247 us
  waiting for transfers between devices  85 us (34%)
  other arithmetic  57.8 us (23%)
  blocking collectives  55.5 us (22%)
  local copies, waits for them, and re-layouts  19.6 us (8%)
  between operations  15.6 us (6%)
  starting transfers between devices  7.96 us (3%)
  matrix products  5.86 us (2%)
    psum x1, waiting for transfers between devices, body(): gram_all, cross = lax.psum((gram_block, cross_block), 'space')  46.2 us
    psum x1, waiting for transfers between devices, body(): gram_block, cross_block = lax.psum((gram_loc, cross_loc), 'member')  37.1 us
    another operation x6, other arithmetic, body(): lower_factor = jnp.linalg.cholesky(cov_matrix)  34 us
    all_to_all x1, blocking collectives, body(): lax.all_to_all(updated_sample.reshape(prior_sample_full.shape), 'member',...  28.2 us
    psum x1, blocking collectives, body(): gram_all, cross = lax.psum((gram_block, cross_block), 'space')  21.5 us
    another operation x3, other arithmetic, solve_lower(): lax.linalg.triangular_solve(lower_factor, target, left_side=True, lower=T...  19.9 us
    unnamed x6, local copies, waits for them, and re-layouts  6.3 us
    psum x1, blocking collectives, body(): gram_block, cross_block = lax.psum((gram_loc, cross_loc), 'member')  5.79 us
  transfers between devices with their start and end apart: 4, of which 3 were waited for; matrix products, arithmetic and copies ran while one was open for 27% of the time, Pallas kernels for 0%

commit v1 on v0

--- a/solution.py
+++ b/solution.py
@@ -1,8 +1,11 @@
+import functools
 import math
 
 import jax
 import jax.numpy as jnp
 from jax import lax
+from jax.experimental import pallas as pl
+from jax.experimental.pallas import tpu as pltpu
 from jax.sharding import PartitionSpec as P
 
 
@@ -10,7 +13,7 @@
     return lax.linalg.triangular_solve(lower_factor, target, left_side=True, lower=True)
 
 
-def body(
+def general_body(
     prior_sample,
     measured_point_location,
     measured_data,
@@ -71,6 +74,391 @@
     return returned.reshape(anomaly_matrix, points_in_region)
 
 
+MESH = pl.DeviceIdType.MESH
+VMEM_SPEC = pl.BlockSpec(memory_space=pltpu.VMEM)
+LANES = 128
+SUBLANES = 8
+
+
+def split2(x):
+    high = x.astype(jnp.bfloat16)
+    low = (x - high.astype(jnp.float32)).astype(jnp.bfloat16)
+    return high, low
+
+
+def dot3(a, b, dims=((1,), (0,))):
+    ah, al = split2(a)
+    bh, bl = split2(b)
+    d = functools.partial(
+        lax.dot_general, dimension_numbers=(dims, ((), ())), preferred_element_type=jnp.float32
+    )
+    return (d(ah, bl) + d(al, bh)) + d(ah, bh)
+
+
+def gather_kernel(x_ref, idx_ref, out_ref, acc_ref):
+    step = pl.program_id(0)
+    members, points = x_ref.shape
+    slots = out_ref.shape[1]
+    x = x_ref[...]
+    high, rest = x.astype(jnp.bfloat16), None
+    rest = x - high.astype(jnp.float32)
+    mid = rest.astype(jnp.bfloat16)
+    low = (rest - mid.astype(jnp.float32)).astype(jnp.bfloat16)
+    parts = jnp.concatenate([high, mid, low], axis=0)
+    index = jnp.concatenate([idx_ref[i : i + 1, :] for i in range(idx_ref.shape[0])], axis=1)
+    where = lax.broadcasted_iota(jnp.int32, (points, slots), 0) + step * points
+    hot = (where == index).astype(jnp.float32).astype(jnp.bfloat16)
+    got = jnp.dot(parts, hot, preferred_element_type=jnp.float32)
+
+    @pl.when(step == 0)
+    def _():
+        acc_ref[...] = got
+
+    @pl.when(step > 0)
+    def _():
+        acc_ref[...] += got
+
+    @pl.when(step == pl.num_programs(0) - 1)
+    def _():
+        total = acc_ref[...]
+        out_ref[...] = (total[:members] + total[members : 2 * members]) + total[2 * members :]
+
+
+def gather_observed(prior, index, tile=1024):
+    members, points = prior.shape
+    slots = index.size
+    return pl.pallas_call(
+        gather_kernel,
+        grid=(points // tile,),
+        out_shape=jax.ShapeDtypeStruct((members, slots), jnp.float32),
+        in_specs=[
+            pl.BlockSpec((members, tile), lambda i: (0, i)),
+            pl.BlockSpec(index.shape, lambda i: (0, 0)),
+        ],
+        out_specs=pl.BlockSpec((members, slots), lambda i: (0, 0)),
+        scratch_shapes=[pltpu.VMEM((3 * members, slots), jnp.float32)],
+    )(prior, index)
+
+
+def flat_row(ref):
+    return jnp.concatenate([ref[i : i + 1, :] for i in range(ref.shape[0])], axis=1)
+
+
+def gram_kernel(
+    spaces,
+    ev_ref,
+    data_ref,
+    sigma_ref,
+    used_ref,
+    out_ref,
+    ev_all,
+    gram,
+    parts,
+    total,
+    ex_send,
+    ex_recv,
+    rs_send,
+    rs_recv,
+    ag_send,
+    ag_recv,
+    fin_send,
+    fin_recv,
+):
+    rank = lax.axis_index("member")
+    place = lax.axis_index("space")
+    rows, slots = ev_ref.shape
+    samples = ev_all.shape[0]
+    chunk = rows // spaces
+    side = rank + 1 - 2 * lax.rem(rank, 2)
+    across = lax.rem(rank + 2, 4)
+
+    barrier = pltpu.get_barrier_semaphore()
+    for other in (side, across):
+        pl.semaphore_signal(
+            barrier, inc=1, device_id={"member": other, "space": place}, device_id_type=MESH
+        )
+    for d in range(1, spaces):
+        pl.semaphore_signal(
+            barrier,
+            inc=1,
+            device_id={"member": rank, "space": lax.rem(place + d, spaces)},
+            device_id_type=MESH,
+        )
+    pl.semaphore_wait(barrier, spaces + 1)
+
+    def send(src, dst, ssem, rsem, member, space):
+        copy = pltpu.make_async_remote_copy(
+            src_ref=src,
+            dst_ref=dst,
+            send_sem=ssem,
+            recv_sem=rsem,
+            device_id={"member": member, "space": space},
+            device_id_type=MESH,
+        )
+        copy.start()
+        return copy
+
+    def member_rows(ref, member):
+        return ref.at[pl.ds(pl.multiple_of(member * rows, SUBLANES), rows)]
+
+    def exchange(source, full, ssem, rsem):
+        far = send(source, member_rows(full, rank), ssem.at[0], rsem.at[0], across, place)
+        near = send(source, member_rows(full, rank), ssem.at[1], rsem.at[1], side, place)
+        far.wait_recv()
+        got = member_rows(full, across)
+        relay = send(got, got, ssem.at[2], rsem.at[2], side, place)
+        near.wait_recv()
+        relay.wait_recv()
+        return (far, near, relay)
+
+    pending = exchange(ev_ref, ev_all, ex_send, ex_recv)
+    own = pl.ds(pl.multiple_of(rank * rows, SUBLANES), rows)
+    ev_all[own, :] = ev_ref[...]
+
+    slot = lax.broadcasted_iota(jnp.int32, (1, slots), 1)
+    weight = jnp.where(slot < used_ref[0], 1.0 / flat_row(sigma_ref), 0.0)
+    ev = ev_all[...]
+    mean = jnp.sum(ev, axis=0, keepdims=True) * (1.0 / samples)
+    anomalies = (ev - mean) * weight
+    innovation = (flat_row(data_ref) - mean) * weight
+    first = lax.broadcasted_iota(jnp.int32, (LANES, slots), 0) == 0
+    extra = jnp.where(first, jnp.broadcast_to(innovation, (LANES, slots)), 0.0)
+    mine = (ev_ref[...] - mean) * weight
+    right = jnp.concatenate([anomalies, extra], axis=0)
+    gram[...] = dot3(mine, right, ((1,), (1,)))
+
+    copies = []
+    for d in range(1, spaces):
+        other = lax.rem(place + d, spaces)
+        copies.append(
+            send(
+                gram.at[pl.ds(pl.multiple_of(other * chunk, SUBLANES), chunk)],
+                parts.at[d - 1],
+                rs_send.at[d - 1],
+                rs_recv.at[d - 1],
+                rank,
+                other,
+            )
+        )
+    acc = gram[pl.ds(pl.multiple_of(place * chunk, SUBLANES), chunk), :]
+    for d in range(1, spaces):
+        copies[d - 1].wait_recv()
+        acc = acc + parts[d - 1]
+    piece = pl.ds(pl.multiple_of(rank * rows + place * chunk, SUBLANES), chunk)
+    total[piece, :] = acc
+    spread = []
+    for d in range(1, spaces):
+        other = lax.rem(place + d, spaces)
+        spread.append(
+            send(
+                total.at[piece], total.at[piece], ag_send.at[d - 1], ag_recv.at[d - 1], rank, other
+            )
+        )
+    for copy in spread:
+        copy.wait_recv()
+    last = exchange(member_rows(total, rank), total, fin_send, fin_recv)
+    for copy in (*pending, *copies, *spread, *last):
+        copy.wait_send()
+    out_ref[...] = total[...]
+
+
+def summed_gram(ev, data, sigma, used, members, spaces):
+    rows, slots = ev.shape
+    samples = rows * members
+    width = samples + LANES
+    dma = pltpu.SemaphoreType.DMA
+    return pl.pallas_call(
+        functools.partial(gram_kernel, spaces),
+        out_shape=jax.ShapeDtypeStruct((samples, width), jnp.float32),
+        in_specs=[VMEM_SPEC] * 3 + [pl.BlockSpec(memory_space=pltpu.SMEM)],
+        out_specs=VMEM_SPEC,
+        scratch_shapes=[
+            pltpu.VMEM((samples, slots), jnp.float32),
+            pltpu.VMEM((rows, width), jnp.float32),
+            pltpu.VMEM((spaces - 1, rows // spaces, width), jnp.float32),
+            pltpu.VMEM((samples, width), jnp.float32),
+            dma((3,)),
+            dma((3,)),
+            dma((spaces - 1,)),
+            dma((spaces - 1,)),
+            dma((spaces - 1,)),
+            dma((spaces - 1,)),
+            dma((3,)),
+            dma((3,)),
+        ],
+        compiler_params=pltpu.CompilerParams(collective_id=0, has_side_effects=True),
+    )(ev, data, sigma, used)
+
+
+PIVOTS = 4
+
+
+def inverse_factor(a):
+    size = a.shape[0]
+    count = size // SUBLANES
+    shape = (SUBLANES, size)
+    m = [a[SUBLANES * i : SUBLANES * (i + 1), :] for i in range(count)]
+    diag = [None] * count
+    lane = lax.broadcasted_iota(jnp.int32, shape, 1)
+    sub = lax.broadcasted_iota(jnp.int32, shape, 0)
+
+    def column(x, k):
+        return jnp.broadcast_to(x[:, k : k + 1], shape)
+
+    def row(x, r):
+        return jnp.broadcast_to(x[r : r + 1, :], shape)
+
+    for k in range(0, size, PIVOTS):
+        t, r = divmod(k, SUBLANES)
+        inside = (lane >= k) & (lane < k + PIVOTS)
+        cols = [column(m[t], k + q) for q in range(PIVOTS)]
+        pivot = {(q, p): row(cols[p], r + q) for p in range(PIVOTS) for q in range(p, PIVOTS)}
+        base = [
+            jnp.where(inside, jnp.where(lane == k + q, 1.0, 0.0), row(m[t], r + q))
+            for q in range(PIVOTS)
+        ]
+        inverse = []
+        for p in range(PIVOTS):
+            inverse.append(1.0 / pivot[p, p])
+            for q in range(p + 1, PIVOTS):
+                factor = pivot[q, p] * inverse[p]
+                base[q] = base[q] - factor * base[p]
+                for s in range(q, PIVOTS):
+                    pivot[s, q] = pivot[s, q] - factor * pivot[s, p]
+        for p in range(PIVOTS):
+            old = diag[t]
+            diag[t] = pivot[p, p] if old is None else jnp.where(sub >= r + p, pivot[p, p], old)
+        for i in range(t, count):
+            cols_i = cols if i == t else [column(m[i], k + q) for q in range(PIVOTS)]
+            cols_i = list(cols_i)
+            if i == t:
+                unit = jnp.where(lane - k == sub - r, 1.0, 0.0)
+                x = jnp.where(inside & (sub >= r), unit, m[i])
+            else:
+                x = jnp.where(inside, 0.0, m[i])
+            for p in range(PIVOTS):
+                mult = cols_i[p] * inverse[p]
+                if i == t:
+                    mult = jnp.where(sub > r + p, mult, 0.0)
+                for q in range(p + 1, PIVOTS):
+                    cols_i[q] = cols_i[q] - mult * pivot[q, p]
+                x = x - mult * base[p]
+            m[i] = x
+    out = []
+    for i in range(count):
+        keep = lane <= sub + SUBLANES * i
+        out.append(jnp.where(keep, m[i] * lax.rsqrt(diag[i]), 0.0))
+    return jnp.concatenate(out, axis=0)
+
+
+def eye_mask(rows, cols):
+    shape = (rows, cols)
+    return lax.broadcasted_iota(jnp.int32, shape, 0) == lax.broadcasted_iota(jnp.int32, shape, 1)
+
+
+def transform_kernel(g_ref, out_ref, inv_ref):
+    samples = g_ref.shape[0]
+    b = LANES
+    ridge = float(samples - 1)
+    n = samples // b
+    work = {}
+    for i in range(n):
+        for j in range(i + 1):
+            block = g_ref[i * b : (i + 1) * b, j * b : (j + 1) * b]
+            work[i, j] = block + jnp.where(eye_mask(b, b), ridge, 0.0) if i == j else block
+    inv = {}
+    low = {}
+    for k in range(n):
+        inv[k, k] = inverse_factor(work[k, k])
+        for i in range(k + 1, n):
+            low[i, k] = dot3(work[i, k], inv[k, k], ((1,), (1,)))
+        for i in range(k + 1, n):
+            for j in range(k + 1, i + 1):
+                work[i, j] = work[i, j] - dot3(low[i, k], low[j, k], ((1,), (1,)))
+        for j in range(k):
+            acc = dot3(low[k, j], inv[j, j])
+            for s in range(j + 1, k):
+                acc = acc + dot3(low[k, s], inv[s, j])
+            inv[k, j] = -dot3(inv[k, k], acc)
+    zero = jnp.zeros((b, b), jnp.float32)
+    full = jnp.concatenate(
+        [
+            jnp.concatenate([inv[i, j] if j <= i else zero for j in range(n)], axis=1)
+            for i in range(n)
+        ],
+        axis=0,
+    )
+    inv_ref[...] = full
+    cross = g_ref[:, samples : samples + b]
+    projected = dot3(full, cross)
+    mean_weight = jnp.sum(full * projected[:, 0:1], axis=0, keepdims=True)
+    out_ref[...] = math.sqrt(samples - 1) * full + mean_weight
+
+
+def transform_of(gram):
+    samples = gram.shape[0]
+    return pl.pallas_call(
+        transform_kernel,
+        out_shape=jax.ShapeDtypeStruct((samples, samples), jnp.float32),
+        in_specs=[VMEM_SPEC],
+        out_specs=VMEM_SPEC,
+        scratch_shapes=[pltpu.VMEM((samples, samples), jnp.float32)],
+        cost_estimate=pl.CostEstimate(
+            flops=40_000_000, bytes_accessed=4 * samples * samples * 40, transcendentals=0
+        ),
+    )(gram)
+
+
+def analysis_kernel(t_ref, own_ref, side_ref, across_ref, both_ref, out_ref, x_ref):
+    rank = lax.axis_index("member")
+    rows = own_ref.shape[0]
+    samples = x_ref.shape[0]
+    side = rank + 1 - 2 * lax.rem(rank, 2)
+    across = lax.rem(rank + 2, 4)
+    both = lax.rem(side + 2, 4)
+    pieces = ((rank, own_ref), (side, side_ref), (across, across_ref), (both, both_ref))
+    total = None
+    for member, ref in pieces:
+        part = jnp.sum(ref[...], axis=0, keepdims=True)
+        total = part if total is None else total + part
+    mean = total * (1.0 / samples)
+    for member, ref in pieces:
+        x_ref[pl.ds(pl.multiple_of(member * rows, SUBLANES), rows), :] = ref[...] - mean
+    mine = t_ref[pl.ds(pl.multiple_of(rank * rows, SUBLANES), rows), :]
+    out_ref[...] = mean + dot3(mine, x_ref[...])
+
+
+def analysis_rows(transform, pieces, tile=1024):
+    rows, points = pieces[0].shape
+    samples = transform.shape[0]
+    block = pl.BlockSpec((rows, tile), lambda i: (0, i))
+    return pl.pallas_call(
+        analysis_kernel,
+        grid=(points // tile,),
+        out_shape=jax.ShapeDtypeStruct((rows, points), jnp.float32),
+        in_specs=[pl.BlockSpec((samples, samples), lambda i: (0, 0))] + [block] * 4,
+        out_specs=block,
+        scratch_shapes=[pltpu.VMEM((samples, tile), jnp.float32)],
+    )(transform, *pieces)
+
+
+def body(prior_sample, location, data, sigma, used):
+    rows, points = prior_sample.shape
+    members = lax.axis_size("member")
+    spaces = lax.axis_size("space")
+    if members != 4 or rows % (SUBLANES * spaces) or (rows * members) % LANES:
+        return general_body(prior_sample, location, data, sigma, used)
+    near = [(i, i ^ 1) for i in range(members)]
+    far = [(i, i ^ 2) for i in range(members)]
+    across = lax.ppermute(prior_sample, "member", far)
+    side = lax.ppermute(prior_sample, "member", near)
+    both = lax.ppermute(across, "member", near)
+    observed = gather_observed(prior_sample, location)
+    gram = summed_gram(observed, data, sigma, used, members, spaces)
+    transform = transform_of(gram)
+    return analysis_rows(transform, (prior_sample, side, across, both))
+
+
 def solution(mesh):
     placed = (
         P("member", "space"),

time: 248 us -> 106 us (0.43)
  other arithmetic: 57.8 us -> 0 us
  Pallas kernels: 0 us -> 56.3 us
  blocking collectives: 55.5 us -> 0 us
  waiting for transfers between devices: 85 us -> 45.8 us
  local copies, waits for them, and re-layouts: 19.6 us -> 0.01 us
  between operations: 15.6 us -> 0.67 us
  matrix products: 5.86 us -> 0 us
  starting transfers between devices: 7.96 us -> 3 us
    psum x2 -> x0, waiting for transfers between devices: 83.3 us -> none  [the longest x1 46.2 us: body(): gram_all, cross = lax.psum((gram_block, cross_block), 'space')]
    pallas_call x0 -> x4, Pallas kernels: none -> 56.3 us  [the longest x1 26.6 us: summed_gram(): pl.pallas_call(functools.partial(gram_kernel, spaces), out_shape=jax.Shap...]
    another operation x9 -> x0, other arithmetic: 53.9 us -> none  [the longest x6 34 us: body(): lower_factor = jnp.linalg.cholesky(cov_matrix)]
    ppermute x0 -> x3, waiting for transfers between devices: none -> 45.8 us  [the longest x1 45.8 us: body(): across = lax.ppermute(prior_sample, 'member', far)]
    all_to_all x1 -> x0, blocking collectives: 28.2 us -> none  [body(): lax.all_to_all(updated_sample.reshape(prior_sample_full.shape), 'member',...]
    psum x2 -> x0, blocking collectives: 27.3 us -> none  [the longest x1 21.5 us: body(): gram_all, cross = lax.psum((gram_block, cross_block), 'space')]
    all_to_all x2 -> x0, starting transfers between devices: 7.87 us -> none  [the longest x1 4.26 us: body(): lax.all_to_all(propagated_grid, 'member', split_axis=1, concat_axis=0, ti...]
    unnamed x6 -> x2, local copies, waits for them, and re-layouts: 6.3 us -> 0.01 us
  transfers between devices with their start and end apart: 4 -> 3, of which waited for: 3 -> 1; matrix products, arithmetic and copies ran while one was open for 27% -> 0% of each run, Pallas kernels for 0% -> 44%
where the time goes in v1:
time: 106 us
  Pallas kernels  56.3 us (53%)
  waiting for transfers between devices  45.8 us (43%)
  starting transfers between devices  3 us (3%)
    ppermute x1, waiting for transfers between devices, body(): across = lax.ppermute(prior_sample, 'member', far)  45.8 us
    pallas_call x1, Pallas kernels, summed_gram(): pl.pallas_call(functools.partial(gram_kernel, spaces), out_shape=jax.Shap...  26.6 us
    pallas_call x1, Pallas kernels, transform_of(): pl.pallas_call(transform_kernel, out_shape=jax.ShapeDtypeStruct((samples,...  13.7 us
    pallas_call x1, Pallas kernels, analysis_rows(): pl.pallas_call(analysis_kernel, grid=(points // tile,), out_shape=jax.Sha...  9.28 us
    pallas_call x1, Pallas kernels, gather_observed(): pl.pallas_call(gather_kernel, grid=(points // tile,), out_shape=jax.Shape...  6.72 us
    ppermute x1, starting transfers between devices, body(): across = lax.ppermute(prior_sample, 'member', far)  3 us
  transfers between devices with their start and end apart: 3, of which 1 were waited for; matrix products, arithmetic and copies ran while one was open for 0% of the time, Pallas kernels for 44%

profile of v1, /device:TPU:0, one launch (start us, length us, event | category | flops | bytes accessed | tf_op | source)
XLA Modules:
  0.0 105.8 jit_solution(366113165263371035)
XLA Ops:
  0.0 3.0 %collective-permute-start.1 = (f32[64,8192]{1,0:T(8,128)}, f32[64,8192]{1,0:T(8,128)S(1)}, u32[]{:S(2)}, u32[]{:S(2)}) collective-permute-start(f32[64,8192]{1,0:T(8,128)} %own_ref.1), channel_id=1, source_target_pairs={{0,16},{8,24},{16,0},{24,8},{1,17},{9,25},{17,1},{25,9},{2,18},{10... | collective-permute-start | bytes 6291464 | tf_op jit(solution)/shard_map/ppermute | solution.py:453
  3.0 0.0 collective-permute-start
  3.0 45.8 %collective-permute-done.1.across_ref = f32[64,8192]{1,0:T(8,128)S(1)} collective-permute-done((f32[64,8192]{1,0:T(8,128)}, f32[64,8192]{1,0:T(8,128)S(1)}, u32[]{:S(2)}, u32[]{:S(2)}) %collective-permute-start.1) | collective-permute-done | bytes 2097184 | tf_op jit(solution)/shard_map/ppermute | solution.py:453
  48.8 0.0 copy-start
  48.8 0.0 collective-permute-start.2
  49.5 6.7 %shard_map.55.ev_ref = f32[64,512]{1,0:T(8,128)} custom-call(f32[64,8192]{1,0:T(8,128)} %own_ref.1, s32[4,128]{1,0:T(4,128)} %idx_ref.1), custom_call_target="tpu_custom_call" | custom-call | tf_op jit(solution)/shard_map/pallas_call | solution.py:130
  56.2 26.6 %shard_map.56.g_ref = f32[256,384]{1,0:T(8,128)} custom-call(f32[64,512]{1,0:T(8,128)} %shard_map.55.ev_ref, f32[4,128]{1,0:T(4,128)} %data_ref.1, f32[4,128]{1,0:T(4,128)} %sigma_ref.1, s32[1]{0:T(128)S(6)} %copy.6.used_ref), custom_call_target="tpu_custom_call" | custom-call | tf_op jit(solution)/shard_map/pallas_call | solution.py:270
  82.8 13.7 %shard_map.57.t_ref = f32[256,256]{1,0:T(8,128)} custom-call(f32[256,384]{1,0:T(8,128)} %shard_map.56.g_ref), custom_call_target="tpu_custom_call" | custom-call | flops 40000000 | bytes 10485760 | tf_op jit(solution)/shard_map/pallas_call | solution.py:400
  96.5 0.0 collective-permute-done.side_ref
  96.5 0.0 collective-permute-done.2.both_ref
  96.5 0.0 copy-done
  96.5 9.3 %shard_map.58 = f32[64,8192]{1,0:T(8,128)} custom-call(f32[256,256]{1,0:T(8,128)} %shard_map.57.t_ref, f32[64,8192]{1,0:T(8,128)} %own_ref.1, f32[64,8192]{1,0:T(8,128)} %collective-permute-done.side_ref, f32[64,8192]{1,0:T(8,128)} %copy-done, f32[64,8192]{1,0:T(8,128)} %collective-permute-done.2.both_ref), custom_call_target="tpu_custom_call" | custom-call | tf_op jit(solution)/shard_map/pallas_call | solution.py:435
Async XLA Ops:
  0.0 48.8 %collective-permute-start.1 = (f32[64,8192]{1,0:T(8,128)}, f32[64,8192]{1,0:T(8,128)S(1)}, u32[]{:S(2)}, u32[]{:S(2)}) collective-permute-start(f32[64,8192]{1,0:T(8,128)} %own_ref.1), channel_id=1, source_target_pairs={{0,16},{8,24},{16,0},{24,8},{1,17},{9,25},{17,1},{25,9},{2,18},{10... | collective-permute-start | bytes 6291464 | tf_op jit(solution)/shard_map/ppermute | solution.py:453
  3.0 93.5 %collective-permute-start = (f32[64,8192]{1,0:T(8,128)}, f32[64,8192]{1,0:T(8,128)}, u32[]{:S(2)}, u32[]{:S(2)}) collective-permute-start(f32[64,8192]{1,0:T(8,128)} %own_ref.1), channel_id=1, source_target_pairs={{0,8},{8,0},{16,24},{24,16},{1,9},{9,1},{17,25},{25,17},{2,10},{10... | collective-permute-start | bytes 6291464 | tf_op jit(solution)/shard_map/ppermute | solution.py:454
  48.8 47.7 %copy-start = (f32[64,8192]{1,0:T(8,128)}, f32[64,8192]{1,0:T(8,128)S(1)}, u32[]{:S(2)}) copy-start(f32[64,8192]{1,0:T(8,128)S(1)} %collective-permute-done.1.across_ref) | copy-start | bytes 6291460
  48.8 47.7 %collective-permute-start.2 = (f32[64,8192]{1,0:T(8,128)S(1)}, f32[64,8192]{1,0:T(8,128)}, u32[]{:S(2)}, u32[]{:S(2)}) collective-permute-start(f32[64,8192]{1,0:T(8,128)S(1)} %collective-permute-done.1.across_ref), channel_id=1, source_target_pairs={{0,8},{8,0},{16,24},{24,16},{1,9},{9,1},{17,25},{25,17},{2,10},{10... | collective-permute-start | bytes 6291464 | tf_op jit(solution)/shard_map/ppermute | solution.py:455
